TPU v7x, 32 devices: a whole 2x2x4 slice. The times are simulated.
32 devices in a mesh: dp: 2 (over y), tm: 8 (over z, core), height: 2 (over x).
Axes of the slice: x: 2, y: 2, z: 4, core: 2. Of those that a mesh axis runs over, the one named last changes fastest.
Arguments:
- clip_input: bfloat16 [2, 32, 8, 96, 128], P('dp', 'tm', 'height'), may hold values from -6 to 6
- cotangent: bfloat16 [2, 32, 8, 96, 128], P('dp', 'tm', 'height'), may hold values from -6 to 6
- first_kernel: bfloat16 [2592, 96], replicated, may hold values from -0.125 to 0.125
- second_kernel: bfloat16 [2592, 96], replicated, may hold values from -0.125 to 0.125
Outputs:
- block_output: float32 [2, 32, 8, 96, 128], P('dp', 'tm', 'height')
- input_grad: float32 [2, 32, 8, 96, 128], P('dp', 'tm', 'height')
- first_grad: float32 [2592, 96], P('dp')
- second_grad: float32 [2592, 96], P('dp')
All inputs are finite; a program needn't handle non-finite values.
Results may differ from a plain program's by a relative error of at most 0.0048.
Values may be sent and summed in bfloat16 or wider, within the bound.
A program may use at most 64 MiB of HBM per device.

v0:
```python
import functools
import math

import jax
import jax.numpy as jnp
from jax import lax
from jax.experimental import pallas as pl
from jax.experimental.pallas import tpu as pltpu
from jax.sharding import PartitionSpec as P

EPSILON = 1e-06
MESH_IDS = pl.DeviceIdType.MESH


def factor_of(value):
    return lax.rsqrt(jnp.mean(value * value, axis=0, keepdims=True) + EPSILON)


def act(value):
    scaled = value * factor_of(value)
    return scaled / (1.0 + jnp.exp(-scaled))


def act_back(value, grad):
    factor = factor_of(value)
    scaled = value * factor
    gate = 1.0 / (1.0 + jnp.exp(-scaled))
    inner = grad * (gate * (1.0 + scaled * (1.0 - gate)))
    return factor * (inner - scaled * jnp.mean(inner * scaled, axis=0, keepdims=True))


def body(
    sizes,
    x,
    cot,
    kernel_one,
    kernel_two,
    plain_one,
    plain_two,
    block_out,
    input_out,
    total,
    flip_one,
    flip_two,
    acts_one,
    acts_two,
    grads_two,
    grads_one,
    middle,
    second_act,
    middle_grad,
    time_halo,
    row_halo,
    corner_halo,
    terms,
    first,
    wide,
    narrow_dp,
    got_dp,
    narrow_h,
    got_h,
    wide_z,
    narrow_z,
    got_z,
    mine,
    halo_send,
    halo_recv,
    send,
    recv,
):
    dp, heights, depth = sizes
    frames, rows, channels, cols = x.shape
    shards = 2 * depth
    chunk = terms.shape[1] // dp
    shard = lax.axis_index("tm")
    core, level = shard % 2, shard // 2
    clip, half = lax.axis_index("dp"), lax.axis_index("height")
    other = 1 - half
    has_before, has_after = shard > 0, shard < shards - 1
    edge_row = (rows - 1) * other
    halo_row = (rows + 1) * other
    rim_row = (rows + 1) * half

    barrier = pltpu.get_barrier_semaphore()
    partner = {"tm": level * 2 + 1 - core}
    clip_peers = [(clip + step) % dp for step in range(1, dp)]
    level_peers = [(level + step) % depth for step in range(1, depth)]
    places = [partner, {"height": other}]
    places += [{"dp": peer} for peer in clip_peers]
    places += [{"tm": peer * 2 + core} for peer in level_peers]

    def greet(place):
        pl.semaphore_signal(barrier, inc=1, device_id=place, device_id_type=MESH_IDS)

    for place in places:
        greet(place)

    outer = shard + 2 * core - 1
    has_outer = jnp.logical_and(outer >= 0, outer < shards)

    @pl.when(has_outer)
    def _():
        greet({"tm": outer})

    @pl.when(has_before)
    def _():
        greet({"tm": shard - 1, "height": other})

    @pl.when(has_after)
    def _():
        greet({"tm": shard + 1, "height": other})

    near = has_outer.astype(jnp.int32) + has_before.astype(jnp.int32) + has_after.astype(jnp.int32)
    pl.semaphore_wait(barrier, len(places) + near)

    def remote(source, target, sender, receiver, place):
        return pltpu.make_async_remote_copy(
            src_ref=source,
            dst_ref=target,
            send_sem=sender,
            recv_sem=receiver,
            device_id=place,
            device_id_type=MESH_IDS,
        )

    def exchange(own, slot, ahead):
        step = -1 if ahead else 1
        start = 0 if ahead else frames - 2
        goes, comes = (has_before, has_after) if ahead else (has_after, has_before)
        span = pl.ds(start, 2)
        along = remote(own.at[span], time_halo.at[slot], halo_send.at[slot, 0], halo_recv.at[slot, 0], {"tm": shard + step})
        across = remote(own.at[:, edge_row], row_halo.at[slot], halo_send.at[slot, 1], halo_recv.at[slot, 1], {"height": other})
        corner = remote(
            own.at[span, edge_row],
            corner_halo.at[slot],
            halo_send.at[slot, 2],
            halo_recv.at[slot, 2],
            {"tm": shard + step, "height": other},
        )
        across.start()

        @pl.when(goes)
        def _():
            along.start()
            corner.start()

        def arrive():
            across.wait()

            @pl.when(goes)
            def _():
                along.wait_send()
                corner.wait_send()

            @pl.when(comes)
            def _():
                along.wait_recv()
                corner.wait_recv()

        return arrive

    lane = lax.broadcasted_iota(jnp.int32, (channels, cols), 1)

    def place_tile(field, frame, row, value):
        wide_value = value.astype(jnp.float32)
        left = jnp.where(lane == 0, 0.0, pltpu.roll(wide_value, 1, axis=1))
        right = jnp.where(lane == cols - 1, 0.0, pltpu.roll(wide_value, cols - 1, axis=1))
        field[frame, row, 0:channels] = left.astype(jnp.bfloat16)
        field[frame, row, channels : 2 * channels] = value
        field[frame, row, 2 * channels : 3 * channels] = right.astype(jnp.bfloat16)

    def fill_halo(field, slot, ahead, make):
        inside, outside = (0, frames) if ahead else (2, 0)
        comes = has_after if ahead else has_before
        blank = jnp.zeros((3 * channels, cols), jnp.bfloat16)
        for frame in range(frames + 2):
            field[frame, rim_row] = blank

        def row_step(frame, carry):
            place_tile(field, inside + frame, halo_row, make(row_halo[slot, frame]))
            return carry

        lax.fori_loop(0, frames, row_step, 0)

        @pl.when(comes)
        def _():
            def time_step(index, carry):
                frame, row = index // rows, index % rows
                place_tile(field, outside + frame, row + 1, make(time_halo[slot, frame, row]))
                return carry

            lax.fori_loop(0, 2 * rows, time_step, 0)
            for frame in range(2):
                place_tile(field, outside + frame, halo_row, make(corner_halo[slot, frame]))

        @pl.when(jnp.logical_not(comes))
        def _():
            for frame in range(2):
                for row in range(rows + 2):
                    field[outside + frame, row] = blank

    steps = frames // 2 * rows

    def conv(field, kernel, finish, begin=0, end=steps):
        def step(index, carry):
            frame, row = 2 * (index // rows), index % rows
            summed = None
            for tap in range(3):
                pair = [
                    field[frame + tap + side, pl.ds(row, 3)].reshape(9 * channels, cols) for side in range(2)
                ]
                part = jnp.dot(kernel[tap], jnp.concatenate(pair, axis=1), preferred_element_type=jnp.float32)
                summed = part if summed is None else summed + part
            for side in range(2):
                finish(frame + side, row, summed[:, side * cols : (side + 1) * cols])
            return carry

        lax.fori_loop(begin, end, step, 0)

    def kernel_grad(slot, field, grad):
        def step(index, carry):
            tap, tap_row = index // 3, index % 3
            tiles = [(frame, row) for frame in range(frames) for row in range(rows)]
            left = jnp.concatenate([field[frame + tap, row + tap_row] for frame, row in tiles], axis=1)
            right = jnp.concatenate([grad[frame, row] for frame, row in tiles], axis=1)
            piece = lax.dot_general(left, right, (((1,), (1,)), ((), ())), preferred_element_type=jnp.float32)
            terms[slot, pl.ds(pl.multiple_of(index * 3 * channels, 3 * channels), 3 * channels)] = piece
            return carry

        lax.fori_loop(0, 9, step, 0)

    def as_act(value):
        return act(value.astype(jnp.float32)).astype(jnp.bfloat16)

    x_arrives = exchange(x, 0, False)
    cot_arrives = exchange(cot, 1, True)

    def first_step(index, carry):
        frame, row = index // rows, index % rows
        place_tile(acts_one, frame + 2, row + 1, as_act(x[frame, row]))
        place_tile(grads_two, frame, row + 1, cot[frame, row])
        return carry

    lax.fori_loop(0, frames * rows, first_step, 0)
    for plain, flip in ((plain_two, flip_two), (plain_one, flip_one)):
        for index in range(27):
            tile = plain[(26 - index) * channels : (27 - index) * channels]
            flip[index // 9, :, (index % 9) * channels : (index % 9 + 1) * channels] = tile
    x_arrives()
    fill_halo(acts_one, 0, False, as_act)

    def finish_middle(frame, row, value):
        middle[frame, row] = value
        rounded = act(value).astype(jnp.bfloat16)
        second_act[frame, row] = rounded
        place_tile(acts_two, frame + 2, row + 1, rounded)

    conv(acts_one, kernel_one, finish_middle)
    act_arrives = exchange(second_act, 2, False)
    cot_arrives()
    fill_halo(grads_two, 1, True, lambda value: value)

    def finish_back(frame, row, value):
        rounded = act_back(middle[frame, row], value).astype(jnp.bfloat16)
        middle_grad[frame, row] = rounded
        place_tile(grads_one, frame, row + 1, rounded)

    conv(grads_two, flip_two, finish_back)
    grad_arrives = exchange(middle_grad, 3, True)

    used = [0]

    def send_to(source, target, place):
        slot = used[0]
        used[0] += 1
        copy = remote(source, target, send.at[slot], recv.at[slot], place)
        copy.start()
        return copy

    kernel_grad(0, acts_one, middle_grad)
    act_arrives()
    fill_halo(acts_two, 2, False, lambda value: value)
    kernel_grad(1, acts_two, cot)
    swap = send_to(terms.at[1 - core], first, partner)

    def finish_branch(frame, row, value):
        block_out[frame, row] = x[frame, row].astype(jnp.float32) + value

    def finish_input(frame, row, value):
        back = act_back(x[frame, row].astype(jnp.float32), value)
        input_out[frame, row] = cot[frame, row].astype(jnp.float32) + back

    conv(acts_two, kernel_two, finish_branch, 0, steps // 2)
    swap.wait()
    padded = wide.shape[1]
    for index in range(dp):
        span = pl.ds(index * chunk, chunk)
        summed = terms[core, span] + first[span]
        if padded > chunk:
            summed = jnp.concatenate([summed, jnp.zeros((padded - chunk, channels), jnp.float32)], axis=0)
        wide[index] = summed
        narrow_dp[index] = summed.astype(jnp.bfloat16)
    copies = [send_to(narrow_dp.at[peer], got_dp.at[i], {"dp": peer}) for i, peer in enumerate(clip_peers)]
    conv(acts_two, kernel_two, finish_branch, steps // 2, steps)
    grad_arrives()
    fill_halo(grads_one, 3, True, lambda value: value)
    conv(grads_one, flip_one, finish_input, 0, steps // 2)
    for copy in copies:
        copy.wait()
    summed = wide[clip]
    for i in range(dp - 1):
        summed = summed + got_dp[i].astype(jnp.float32)
    wide[0] = summed
    narrow_h[...] = summed.astype(jnp.bfloat16).reshape(narrow_h.shape)
    copy = send_to(narrow_h.at[other], got_h, {"height": other})
    conv(grads_one, flip_one, finish_input, steps // 2, steps)
    copy.wait()
    block = wide_z.shape[1]
    mine_rows = pl.ds(pl.multiple_of(half * (depth * block), depth * block), depth * block)
    summed = wide[0, mine_rows] + got_h[...].astype(jnp.float32)
    wide_z[...] = summed.reshape(wide_z.shape)
    narrow_z[...] = summed.reshape(wide_z.shape).astype(jnp.bfloat16)
    copies = [
        send_to(narrow_z.at[peer], got_z.at[i], {"tm": peer * 2 + core}) for i, peer in enumerate(level_peers)
    ]
    for copy in copies:
        copy.wait()
    summed = wide_z[level]
    for i in range(depth - 1):
        summed = summed + got_z[i].astype(jnp.float32)
    mine[core, half, level] = summed.astype(jnp.bfloat16)
    own = mine.at[core, half, level]
    copies = [send_to(own, own, {"tm": peer * 2 + core}) for peer in level_peers]
    for copy in copies:
        copy.wait()
    own = mine.at[core, half]
    send_to(own, own, {"height": other}).wait()
    own = mine.at[core]
    send_to(own, own, partner).wait()
    total[...] = mine[...].astype(jnp.float32)


def local(clip_input, cotangent, first_kernel, second_kernel):
    dp, heights, depth = (lax.axis_size("dp"), lax.axis_size("height"), lax.axis_size("tm") // 2)
    assert heights == 2
    _, frames, rows, channels, cols = clip_input.shape
    taps = first_kernel.shape[0]

    def forward(kernel):
        split = kernel.reshape(3, 9 * channels, channels)
        return jnp.swapaxes(split, 1, 2)

    chunk = taps // dp
    block = -(-chunk // (heights * depth * 16)) * 16
    padded = heights * depth * block
    copies = 1 + (dp - 1) + 2 + 2 * (depth - 1) + 1
    tile = (channels, cols)
    field = pltpu.VMEM((frames + 2, rows + 2, 3 * channels, cols), jnp.bfloat16)
    own = (frames, rows) + tile
    vmem = pl.BlockSpec(memory_space=pltpu.VMEM)
    block_output, input_grad, total = pl.pallas_call(
        functools.partial(body, (dp, heights, depth)),
        out_shape=(
            jax.ShapeDtypeStruct(own, jnp.float32),
            jax.ShapeDtypeStruct(own, jnp.float32),
            jax.ShapeDtypeStruct((2, heights, depth, block, channels), jnp.float32),
        ),
        in_specs=[vmem] * 6,
        out_specs=(vmem, vmem, vmem),
        scratch_shapes=[
            pltpu.VMEM((3, channels, 9 * channels), jnp.bfloat16),
            pltpu.VMEM((3, channels, 9 * channels), jnp.bfloat16),
            field,
            field,
            field,
            field,
            pltpu.VMEM(own, jnp.float32),
            pltpu.VMEM(own, jnp.bfloat16),
            pltpu.VMEM(own, jnp.bfloat16),
            pltpu.VMEM((4, 2, rows) + tile, jnp.bfloat16),
            pltpu.VMEM((4, frames) + tile, jnp.bfloat16),
            pltpu.VMEM((4, 2) + tile, jnp.bfloat16),
            pltpu.VMEM((2, taps, channels), jnp.float32),
            pltpu.VMEM((taps, channels), jnp.float32),
            pltpu.VMEM((dp, padded, channels), jnp.float32),
            pltpu.VMEM((dp, padded, channels), jnp.bfloat16),
            pltpu.VMEM((dp - 1, padded, channels), jnp.bfloat16),
            pltpu.VMEM((heights, depth * block, channels), jnp.bfloat16),
            pltpu.VMEM((depth * block, channels), jnp.bfloat16),
            pltpu.VMEM((depth, block, channels), jnp.float32),
            pltpu.VMEM((depth, block, channels), jnp.bfloat16),
            pltpu.VMEM((depth - 1, block, channels), jnp.bfloat16),
            pltpu.VMEM((2, heights, depth, block, channels), jnp.bfloat16),
            pltpu.SemaphoreType.DMA((4, 3)),
            pltpu.SemaphoreType.DMA((4, 3)),
            pltpu.SemaphoreType.DMA((copies,)),
            pltpu.SemaphoreType.DMA((copies,)),
        ],
        compiler_params=pltpu.CompilerParams(collective_id=0, has_side_effects=True),
        name="block_step",
    )(
        clip_input[0],
        cotangent[0],
        forward(first_kernel),
        forward(second_kernel),
        first_kernel,
        second_kernel,
    )
    positions = frames * rows * cols * dp * heights * lax.axis_size("tm")
    factor = 1.0 / math.sqrt(positions)
    flat = total.reshape(2, padded, channels)[:, :chunk] * factor
    return (block_output[None], input_grad[None], flat[0], flat[1])


def solution(mesh):
    split = P("dp", "tm", "height", None, None)
    return jax.shard_map(
        local,
        mesh=mesh,
        in_specs=(split, split, P(), P()),
        out_specs=(split, split, P("dp", None), P("dp", None)),
        check_vma=False,
    )
```

profile of v0, /device:TPU:0, one launch (start us, length us, event | category | flops | bytes accessed | tf_op | source)
XLA Modules:
  0.0 80.4 jit_solution(13970808356920959905)
XLA Ops:
  0.6 0.0 copy-start.1
  0.6 0.0 copy-start
  0.7 2.2 %copy.13.plain_one = bf16[2592,96]{1,0:T(8,128)(2,1)} copy(bf16[2592,96]{0,1:T(8,128)(2,1)} %param.6) | data formatting | bytes 995328 | tf_op args[2]
  2.9 0.0 copy-done.1
  2.9 1.1 %copy.14.plain_two = bf16[2592,96]{1,0:T(8,128)(2,1)} copy(bf16[2592,96]{0,1:T(8,128)(2,1)S(1)} %copy-done.1) | data formatting | bytes 995328 | tf_op args[3]
  4.0 0.0 copy-done
  4.0 0.4 reshape.17
  4.4 0.4 reshape.18
  4.8 1.1 %copy_bitcast_fusion = (bf16[3,96,864]{2,1,0:T(8,128)(2,1)}, bf16[3,96,864]{2,1,0:T(8,128)(2,1)}) fusion(bf16[3,864,96]{1,0,2:T(4,128)(2,1)S(1)} %reshape.18, bf16[3,864,96]{1,0,2:T(4,128)(2,1)S(1)} %reshape.17), kind=kLoop, calls=%fused_computation.3 | loop fusion | bytes 1990656 | tf_op jit(solution)/shard_map/transpose | solution.py:351
  5.8 69.4 %block_step.1 = (f32[4,4,96,128]{3,2,1,0:T(8,128)}, f32[4,4,96,128]{3,2,1,0:T(8,128)}, f32[2,2,4,176,96]{4,3,2,1,0:T(8,128)}) custom-call(bf16[4,4,96,128]{3,2,1,0:T(8,128)(2,1)} %bitcast.20, bf16[4,4,96,128]{3,2,1,0:T(8,128)(2,1)} %bitcast.21, bf16[3,96,864]{2,1,0:T(8,128)(2,1)} %get-tuple-element.13.kernel_one, ...), custom_call_target="tpu_custom_call" | custom-call | tf_op jit(solution)/shard_map/block_step/pallas_call | solution.py:361
  75.2 1.4 %slice.12 = f32[2,1296,96]{2,1,0:T(8,128)S(1)} slice(f32[2,1408,96]{2,1,0:T(8,128)} %bitcast.17), slice={[0:2], [0:1296], [0:96]} | slice | bytes 1990656 | tf_op jit(solution)/shard_map/slice | solution.py:411
  76.6 0.4 copy.16
  77.1 0.1 broadcast_multiply_fusion
  77.2 0.0 copy-start.3
  77.2 1.0 %slice_bitcast_fusion = (f32[1296,96]{0,1:T(8,128)}, f32[1296,96]{0,1:T(8,128)}) fusion(f32[2,1296,96]{1,2,0:T(8,128)S(1)} %broadcast_multiply_fusion), kind=kLoop, calls=%fused_computation | loop fusion | bytes 1990656 | tf_op jit(solution)/shard_map/squeeze | solution.py:412
  78.2 0.0 copy-start.2
  78.2 0.4 copy-done.3
  78.6 0.9 %copy.21 = f32[1,4,4,96,128]{4,3,2,1,0:T(8,128)} copy(f32[1,4,4,96,128]{4,3,2,1,0:T(8,128)S(1)} %bitcast.19) | data formatting | bytes 1572864
  79.5 0.0 copy-done.2
  79.5 0.9 %copy.22 = f32[1,4,4,96,128]{4,3,2,1,0:T(8,128)} copy(f32[1,4,4,96,128]{4,3,2,1,0:T(8,128)S(1)} %bitcast.18) | data formatting | bytes 1572864
Async XLA Ops:
  0.6 2.2 %copy-start.1 = (bf16[2592,96]{0,1:T(8,128)(2,1)S(1)}, bf16[2592,96]{0,1:T(8,128)(2,1)}, u32[]{:S(2)}) copy-start(bf16[2592,96]{0,1:T(8,128)(2,1)} %param.7) | copy-start | bytes 1492996
  0.6 3.3 %copy-start = (bf16[2592,96]{0,1:T(8,128)(2,1)S(1)}, bf16[2592,96]{0,1:T(8,128)(2,1)}, u32[]{:S(2)}) copy-start(bf16[2592,96]{0,1:T(8,128)(2,1)} %param.6) | copy-start | bytes 1492996
  77.2 1.5 %copy-start.3 = (f32[4,4,96,128]{3,2,1,0:T(8,128)S(1)}, f32[4,4,96,128]{3,2,1,0:T(8,128)}, u32[]{:S(2)}) copy-start(f32[4,4,96,128]{3,2,1,0:T(8,128)} %get-tuple-element.7) | copy-start | bytes 2359300
  78.2 1.3 %copy-start.2 = (f32[4,4,96,128]{3,2,1,0:T(8,128)S(1)}, f32[4,4,96,128]{3,2,1,0:T(8,128)}, u32[]{:S(2)}) copy-start(f32[4,4,96,128]{3,2,1,0:T(8,128)} %get-tuple-element.8) | copy-start | bytes 2359300
where the time goes:
time: 80.6 us; the launch traced here: 80.4 us
  Pallas kernels  69.4 us (86%)
  local copies, waits for them, and re-layouts  10.3 us (13%)
    pallas_call x1, Pallas kernels, local(): pl.pallas_call(functools.partial(body, (dp, heights, depth)), out_shape=(...  69.4 us
    unnamed x13, local copies, waits for them, and re-layouts  5.94 us

commit v1 on v0

v1 whole, which is shorter than its diff:
```python
import functools
import math

import jax
import jax.numpy as jnp
from jax import lax
from jax.experimental import pallas as pl
from jax.experimental.pallas import tpu as pltpu
from jax.sharding import PartitionSpec as P

EPSILON = 1e-06
MESH_IDS = pl.DeviceIdType.MESH


def factor_of(value):
    return lax.rsqrt(jnp.mean(value * value, axis=0, keepdims=True) + EPSILON)


def act(value):
    scaled = value * factor_of(value)
    return scaled / (1.0 + jnp.exp(-scaled))


def act_back(value, grad):
    factor = factor_of(value)
    scaled = value * factor
    gate = 1.0 / (1.0 + jnp.exp(-scaled))
    inner = grad * (gate * (1.0 + scaled * (1.0 - gate)))
    return factor * (inner - scaled * jnp.mean(inner * scaled, axis=0, keepdims=True))


def body(
    sizes,
    scale,
    x,
    cot,
    turned_one,
    turned_two,
    block_out,
    input_out,
    grad_one,
    grad_two,
    x_own,
    cot_own,
    turned,
    ahead_weights,
    back_weights,
    acts_one,
    acts_two,
    grads_two,
    grads_one,
    middle,
    second_act,
    middle_grad,
    partial,
    block_own,
    input_own,
    grad_own,
    time_halo,
    row_halo,
    corner_halo,
    terms,
    swap_out,
    swap_in,
    wide,
    narrow,
    plane_in,
    wide_half,
    narrow_half,
    half_in,
    wide_z,
    narrow_z,
    got_z,
    mine,
    halo_send,
    halo_recv,
    send,
    recv,
    local_sem,
):
    dp, heights, depth = sizes
    frames, rows, channels, cols = x.shape
    shards = 2 * depth
    chunk = grad_one.shape[1]
    band, width = narrow_z.shape[2:]
    shard = lax.axis_index("tm")
    core, level = shard % 2, shard // 2
    clip, half = lax.axis_index("dp"), lax.axis_index("height")
    other = 1 - half
    has_before, has_after = shard > 0, shard < shards - 1
    edge_row = (rows - 1) * other
    halo_row = (rows + 1) * other
    rim_row = (rows + 1) * half

    barrier = pltpu.get_barrier_semaphore()
    partner = {"tm": level * 2 + 1 - core}
    clip_peers = [(clip + step) % dp for step in range(1, dp)]
    level_peers = [(level + step) % depth for step in range(1, depth)]
    places = [partner, {"height": other}]
    places += [{"dp": peer} for peer in clip_peers]
    places += [{"tm": peer * 2 + core} for peer in level_peers]

    def greet(place):
        pl.semaphore_signal(barrier, inc=1, device_id=place, device_id_type=MESH_IDS)

    for place in places:
        greet(place)

    outer = shard + 2 * core - 1
    has_outer = jnp.logical_and(outer >= 0, outer < shards)

    @pl.when(has_outer)
    def _():
        greet({"tm": outer})

    @pl.when(has_before)
    def _():
        greet({"tm": shard - 1, "height": other})

    @pl.when(has_after)
    def _():
        greet({"tm": shard + 1, "height": other})

    taken = [0]

    def bring(source, target):
        copy = pltpu.make_async_copy(source, target, local_sem.at[taken[0]])
        taken[0] += 1
        copy.start()
        return copy

    inner = pl.ds(2, frames)
    weights_come = [bring(turned_one, turned.at[0]), bring(turned_two, turned.at[1])]
    x_comes = bring(x, x_own)
    cot_comes = bring(cot, cot_own.at[inner])

    near = has_outer.astype(jnp.int32) + has_before.astype(jnp.int32) + has_after.astype(jnp.int32)
    pl.semaphore_wait(barrier, len(places) + near)

    def remote(source, target, sender, receiver, place):
        return pltpu.make_async_remote_copy(
            src_ref=source,
            dst_ref=target,
            send_sem=sender,
            recv_sem=receiver,
            device_id=place,
            device_id_type=MESH_IDS,
        )

    def exchange(own, slot, ahead):
        step = -1 if ahead else 1
        start = 0 if ahead else frames - 2
        goes, comes = (has_before, has_after) if ahead else (has_after, has_before)
        span = pl.ds(start, 2)
        along = remote(own.at[span], time_halo.at[slot], halo_send.at[slot, 0], halo_recv.at[slot, 0], {"tm": shard + step})
        across = remote(own.at[:, edge_row], row_halo.at[slot], halo_send.at[slot, 1], halo_recv.at[slot, 1], {"height": other})
        corner = remote(
            own.at[span, edge_row],
            corner_halo.at[slot],
            halo_send.at[slot, 2],
            halo_recv.at[slot, 2],
            {"tm": shard + step, "height": other},
        )

        def send_time():
            @pl.when(goes)
            def _():
                along.start()
                corner.start()

        def wait_time():
            @pl.when(goes)
            def _():
                along.wait_send()
                corner.wait_send()

            @pl.when(comes)
            def _():
                along.wait_recv()
                corner.wait_recv()

        return across.start, send_time, across.wait, wait_time

    x_rows_go, x_time_goes, x_rows, x_time = exchange(x, 0, False)
    cot_rows_go, cot_time_goes, cot_rows, cot_time = exchange(cot, 1, True)
    x_rows_go()
    x_time_goes()
    cot_rows_go()
    cot_time_goes()

    lane = lax.broadcasted_iota(jnp.int32, (channels, cols), 1)

    def place_tile(field, frame, row, value):
        wide_value = value.astype(jnp.float32)
        left = jnp.where(lane == 0, 0.0, pltpu.roll(wide_value, 1, axis=1))
        right = jnp.where(lane == cols - 1, 0.0, pltpu.roll(wide_value, cols - 1, axis=1))
        field[frame, row, 0:channels] = left.astype(jnp.bfloat16)
        field[frame, row, channels : 2 * channels] = value
        field[frame, row, 2 * channels : 3 * channels] = right.astype(jnp.bfloat16)

    def clear(field, ahead):
        outside = frames if ahead else 0
        blank = jnp.zeros((3 * channels, cols), jnp.bfloat16)
        for frame in range(frames + 2):
            field[frame, rim_row] = blank
        for frame in range(outside, outside + 2):
            for row in range(rows + 2):
                field[frame, row] = blank

    def fill_rows(field, slot, ahead, make):
        inside = 0 if ahead else 2
        for frame in range(frames):
            place_tile(field, inside + frame, halo_row, make(row_halo[slot, frame]))

    def fill_time(field, slot, ahead, make):
        outside = frames if ahead else 0

        @pl.when(has_after if ahead else has_before)
        def _():
            def step(frame, carry):
                for row in range(rows):
                    place_tile(field, outside + frame, row + 1, make(time_halo[slot, frame, row]))
                place_tile(field, outside + frame, halo_row, make(corner_halo[slot, frame]))
                return carry

            lax.fori_loop(0, 2, step, 0)

    def conv(field, weights, order, finish):
        seen = [0] * frames

        def step(frame):
            taps = [tap for tap in range(3) if 0 <= frame - tap < frames]
            least = taps[0]
            patch = jnp.concatenate([field[frame, row : row + 3].reshape(9 * channels, cols) for row in range(rows)], axis=1)
            lines = weights[least * channels : (taps[-1] + 1) * channels]
            part = jnp.dot(lines, patch, preferred_element_type=jnp.float32)
            for tap in taps:
                target = frame - tap
                seen[target] += 1
                for row in range(rows):
                    value = part[(tap - least) * channels : (tap - least + 1) * channels, row * cols : (row + 1) * cols]
                    if seen[target] > 1:
                        value = partial[target, row] + value
                    if seen[target] == 3:
                        finish(target, row, value)
                    else:
                        partial[target, row] = value

        return [functools.partial(step, frame) for frame in order]

    def run(steps):
        for step in steps:
            step()

    def kernel_grad(slot, field, grad):
        tiles = [(frame, row) for frame in range(frames + 2) for row in range(rows)]
        left = jnp.concatenate(
            [jnp.concatenate([grad[frame - tap + 2, row] for frame, row in tiles], axis=1) for tap in range(3)], axis=0
        )
        right = jnp.concatenate([field[frame, row : row + 3].reshape(9 * channels, cols) for frame, row in tiles], axis=1)
        found = lax.dot_general(left, right, (((1,), (1,)), ((), ())), preferred_element_type=jnp.float32)
        span = 9 * channels
        for tap in range(3):
            for piece in range(dp):
                start, stop = max(tap * span, piece * chunk), min((tap + 1) * span, (piece + 1) * chunk)
                if start < stop:
                    value = found[tap * channels : (tap + 1) * channels, start - tap * span : stop - tap * span]
                    terms[slot, piece, :, start - piece * chunk : stop - piece * chunk] = value

    def as_act(value):
        return act(value.astype(jnp.float32)).astype(jnp.bfloat16)

    def same(value):
        return value

    for field, ahead in ((acts_one, False), (acts_two, False), (grads_two, True), (grads_one, True)):
        clear(field, ahead)
    blank_tile = jnp.zeros((channels, cols), jnp.bfloat16)
    for padded in (cot_own, middle_grad):
        for frame in (0, 1, frames + 2, frames + 3):
            for row in range(rows):
                padded[frame, row] = blank_tile

    x_comes.wait()

    def own_acts(frame, carry):
        for row in range(rows):
            place_tile(acts_one, frame + 2, row + 1, as_act(x_own[frame, row]))
        return carry

    lax.fori_loop(0, frames, own_acts, 0)
    for index, copy in enumerate(weights_come):
        copy.wait()
        plain = jnp.transpose(turned[index])
        for tap in range(3):
            lines = slice(tap * channels, (tap + 1) * channels)
            ahead_weights[index, lines] = turned[index, :, tap * 9 * channels : (tap + 1) * 9 * channels]
            last = 26 - 9 * tap
            tiles = [plain[(last - place) * channels : (last - place + 1) * channels] for place in range(9)]
            back_weights[index, lines] = jnp.concatenate(tiles, axis=1)
    cot_comes.wait()

    def own_grads(frame, carry):
        for row in range(rows):
            place_tile(grads_two, frame, row + 1, cot_own[frame + 2, row])
        return carry

    lax.fori_loop(0, frames, own_grads, 0)

    def finish_middle(frame, row, value):
        middle[frame, row] = value
        rounded = act(value).astype(jnp.bfloat16)
        second_act[frame, row] = rounded
        place_tile(acts_two, frame + 2, row + 1, rounded)

    act_rows_go, act_time_goes, act_rows, act_time = exchange(second_act, 2, False)
    x_rows()
    fill_rows(acts_one, 0, False, as_act)
    steps = conv(acts_one, ahead_weights[0], range(frames + 1, -1, -1), finish_middle)
    run(steps[:frames])
    act_time_goes()
    x_time()
    fill_time(acts_one, 0, False, as_act)
    run(steps[frames:])
    act_rows_go()

    def finish_back(frame, row, value):
        rounded = act_back(middle[frame, row], value).astype(jnp.bfloat16)
        middle_grad[frame + 2, row] = rounded
        place_tile(grads_one, frame, row + 1, rounded)

    grad_rows_go, grad_time_goes, grad_rows, grad_time = exchange(middle_grad.at[inner], 3, True)
    cot_rows()
    fill_rows(grads_two, 1, True, same)
    steps = conv(grads_two, back_weights[1], range(frames + 2), finish_back)
    run(steps[:frames])
    grad_time_goes()
    cot_time()
    fill_time(grads_two, 1, True, same)
    run(steps[frames:])
    grad_rows_go()

    used = [0]

    def send_to(source, target, place):
        slot = used[0]
        used[0] += 1
        copy = remote(source, target, send.at[slot], recv.at[slot], place)
        copy.start()
        return copy

    def wait_all(copies):
        for copy in copies:
            copy.wait()

    def reduce(index, plane_first):
        share = channels // 2

        def piece_of(piece, line, owner):
            lines = pl.ds(pl.multiple_of(owner * share + line * band, band), band)
            return terms[index, piece, lines]

        for piece in range(dp):
            for line in range(2):
                value = piece_of(piece, line, 1 - core).astype(jnp.bfloat16)
                for block in range(depth):
                    swap_out[index, piece, line, block] = value[:, block * width : (block + 1) * width]
        swap = send_to(swap_out.at[index], swap_in.at[index], partner)
        yield
        swap.wait()
        for piece in range(dp):
            for line in range(2):
                value = piece_of(piece, line, core)
                for block in range(depth):
                    summed = value[:, block * width : (block + 1) * width]
                    summed = summed + swap_in[index, piece, line, block].astype(jnp.float32)
                    wide[index, piece, line, block] = summed
                    narrow[index, piece, line, block] = summed.astype(jnp.bfloat16)
        if plane_first:
            copies = [
                send_to(narrow.at[index, peer], plane_in.at[index, i], {"dp": peer}) for i, peer in enumerate(clip_peers)
            ]
            yield
            wait_all(copies)
            summed = wide[index, clip]
            for i in range(dp - 1):
                summed = summed + plane_in[index, i].astype(jnp.float32)
            wide_half[index, 0:2] = summed
            narrow_half[index, 0:2] = summed.astype(jnp.bfloat16)
            copy = send_to(narrow_half.at[index, other], half_in.at[index, 0], {"height": other})
            yield
            copy.wait()
            summed = wide_half[index, half] + half_in[index, 0].astype(jnp.float32)
        else:
            copies = [
                send_to(narrow.at[index, piece, other], half_in.at[index, piece], {"height": other}) for piece in range(dp)
            ]
            yield
            wait_all(copies)
            for piece in range(dp):
                summed = wide[index, piece, half] + half_in[index, piece].astype(jnp.float32)
                wide_half[index, piece] = summed
                narrow_half[index, piece] = summed.astype(jnp.bfloat16)
            copies = [
                send_to(narrow_half.at[index, peer], plane_in.at[index, i, 0], {"dp": peer})
                for i, peer in enumerate(clip_peers)
            ]
            yield
            wait_all(copies)
            summed = wide_half[index, clip]
            for i in range(dp - 1):
                summed = summed + plane_in[index, i, 0].astype(jnp.float32)
        wide_z[index] = summed
        narrow_z[index] = summed.astype(jnp.bfloat16)
        copies = [
            send_to(narrow_z.at[index, peer], got_z.at[index, i], {"tm": peer * 2 + core})
            for i, peer in enumerate(level_peers)
        ]
        yield
        wait_all(copies)
        summed = wide_z[index, level]
        for i in range(depth - 1):
            summed = summed + got_z[index, i].astype(jnp.float32)
        mine[index, core, half, level] = summed.astype(jnp.bfloat16)
        own = mine.at[index, core, half, level]
        copies = [send_to(own, own, {"tm": peer * 2 + core}) for peer in level_peers]
        yield
        wait_all(copies)
        own = mine.at[index, core, half]
        copy = send_to(own, own, {"height": other})
        yield
        copy.wait()
        own = mine.at[index, core]
        copy = send_to(own, own, partner)
        yield
        copy.wait()
        for place in range(2):
            for line in range(2):
                top = place * share + line * band
                for block in range(depth):
                    start, stop = block * width, min((block + 1) * width, chunk)
                    if start < stop:
                        value = mine[index, place, line, block].astype(jnp.float32) * scale
                        grad_own[index, top : top + band, start:stop] = value[:, : stop - start]
        copies_out.append(bring(grad_own.at[index], (grad_one, grad_two)[index]))

    copies_out = []

    def finish_branch(frame, row, value):
        block_own[frame, row] = x_own[frame, row].astype(jnp.float32) + value
        if row == rows - 1:
            copies_out.append(bring(block_own.at[frame], block_out.at[frame]))

    def finish_input(frame, row, value):
        back = act_back(x_own[frame, row].astype(jnp.float32), value)
        input_own[frame, row] = cot_own[frame + 2, row].astype(jnp.float32) + back
        if row == rows - 1:
            copies_out.append(bring(input_own.at[frame], input_out.at[frame]))

    kernel_grad(0, acts_one, middle_grad)
    first = reduce(0, True)
    next(first)
    act_rows()
    fill_rows(acts_two, 2, False, same)
    act_time()
    fill_time(acts_two, 2, False, same)
    kernel_grad(1, acts_two, cot_own)
    next(first)
    second = reduce(1, False)
    next(second)
    steps = conv(acts_two, ahead_weights[1], range(frames + 2), finish_branch)
    run(steps[:3])
    next(second)
    run(steps[3:])
    next(first)
    grad_rows()
    fill_rows(grads_one, 3, True, same)
    grad_time()
    fill_time(grads_one, 3, True, same)
    steps = conv(grads_one, back_weights[0], range(frames + 2), finish_input)
    run(steps[:2])
    next(second)
    run(steps[2:4])
    next(first)
    run(steps[4:])
    next(second)
    going = [first, second]
    while going:
        for task in list(going):
            if next(task, 0) == 0:
                going.remove(task)
    wait_all(copies_out)


def local(clip_input, cotangent, first_kernel, second_kernel):
    dp, heights, depth = (lax.axis_size("dp"), lax.axis_size("height"), lax.axis_size("tm") // 2)
    assert heights == 2
    _, frames, rows, channels, cols = clip_input.shape
    taps = first_kernel.shape[0]
    chunk = taps // dp
    band = channels // 4
    width = -(-chunk // (cols * depth)) * cols
    sends = 2 * (1 + (dp - 1) + max(1, dp) + 2 * (depth - 1) + 2)
    tile = (channels, cols)
    own = (frames, rows) + tile
    block = (depth, band, width)
    anywhere = pl.BlockSpec(memory_space=pl.ANY)
    field = pltpu.VMEM((frames + 2, rows + 2, 3 * channels, cols), jnp.bfloat16)
    padded = pltpu.VMEM((frames + 4, rows) + tile, jnp.bfloat16)
    weights = pltpu.VMEM((2, 3 * channels, 9 * channels), jnp.bfloat16)
    positions = frames * rows * cols * dp * heights * lax.axis_size("tm")
    block_output, input_grad, grad_one, grad_two = pl.pallas_call(
        functools.partial(body, (dp, heights, depth), 1.0 / math.sqrt(positions)),
        out_shape=(
            jax.ShapeDtypeStruct(own, jnp.float32),
            jax.ShapeDtypeStruct(own, jnp.float32),
            jax.ShapeDtypeStruct((channels, chunk), jnp.float32),
            jax.ShapeDtypeStruct((channels, chunk), jnp.float32),
        ),
        in_specs=[anywhere] * 4,
        out_specs=(anywhere,) * 4,
        scratch_shapes=[
            pltpu.VMEM(own, jnp.bfloat16),
            padded,
            pltpu.VMEM((2, channels, taps), jnp.bfloat16),
            weights,
            weights,
            field,
            field,
            field,
            field,
            pltpu.VMEM(own, jnp.float32),
            pltpu.VMEM(own, jnp.bfloat16),
            padded,
            pltpu.VMEM(own, jnp.float32),
            pltpu.VMEM(own, jnp.float32),
            pltpu.VMEM(own, jnp.float32),
            pltpu.VMEM((2, channels, chunk), jnp.float32),
            pltpu.VMEM((4, 2, rows) + tile, jnp.bfloat16),
            pltpu.VMEM((4, frames) + tile, jnp.bfloat16),
            pltpu.VMEM((4, 2) + tile, jnp.bfloat16),
            pltpu.VMEM((2, dp, channels, depth * width), jnp.float32),
            pltpu.VMEM((2, dp, 2) + block, jnp.bfloat16),
            pltpu.VMEM((2, dp, 2) + block, jnp.bfloat16),
            pltpu.VMEM((2, dp, 2) + block, jnp.float32),
            pltpu.VMEM((2, dp, 2) + block, jnp.bfloat16),
            pltpu.VMEM((2, dp - 1, 2) + block, jnp.bfloat16),
            pltpu.VMEM((2, max(2, dp)) + block, jnp.float32),
            pltpu.VMEM((2, max(2, dp)) + block, jnp.bfloat16),
            pltpu.VMEM((2, dp) + block, jnp.bfloat16),
            pltpu.VMEM((2,) + block, jnp.float32),
            pltpu.VMEM((2,) + block, jnp.bfloat16),
            pltpu.VMEM((2, depth - 1, band, width), jnp.bfloat16),
            pltpu.VMEM((2, 2, 2) + block, jnp.bfloat16),
            pltpu.SemaphoreType.DMA((4, 3)),
            pltpu.SemaphoreType.DMA((4, 3)),
            pltpu.SemaphoreType.DMA((sends,)),
            pltpu.SemaphoreType.DMA((sends,)),
            pltpu.SemaphoreType.DMA((6 + 2 * frames,)),
        ],
        compiler_params=pltpu.CompilerParams(collective_id=0, has_side_effects=True),
        name="block_step",
    )(clip_input[0], cotangent[0], first_kernel.T, second_kernel.T)
    return (block_output[None], input_grad[None], grad_one.T, grad_two.T)


def solution(mesh):
    split = P("dp", "tm", "height", None, None)
    return jax.shard_map(
        local,
        mesh=mesh,
        in_specs=(split, split, P(), P()),
        out_specs=(split, split, P("dp", None), P("dp", None)),
        check_vma=False,
    )
```

time: 80.6 us -> 51.5 us (0.64)
  Pallas kernels: 69.4 us -> 45.1 us
  local copies, waits for them, and re-layouts: 10.3 us -> 5.52 us
    pallas_call x1, Pallas kernels: 69.4 us -> 45.1 us  [local(): pl.pallas_call(functools.partial(body, (dp, heights, depth), 1.0 / math.s...]
    slice x1 -> x0, local copies, waits for them, and re-layouts: 1.41 us -> none  [local(): flat = total.reshape(2, padded, channels)[:, :chunk] * factor]
    transpose x1 -> x0, local copies, waits for them, and re-layouts: 1.07 us -> none  [forward(): return jnp.swapaxes(split, 1, 2)]
    squeeze x1 -> x0, local copies, waits for them, and re-layouts: 1.05 us -> none  [local(): return (block_output[None], input_grad[None], flat[0], flat[1])]
    unnamed x13 -> x10, local copies, waits for them, and re-layouts: 5.94 us -> 5.52 us
where the time goes in v1:
time: 51.5 us; the launch traced here: 51.3 us
  Pallas kernels  45.1 us (88%)
  local copies, waits for them, and re-layouts  5.52 us (11%)
  between operations  0.65 us (1%)
    pallas_call x1, Pallas kernels, local(): pl.pallas_call(functools.partial(body, (dp, heights, depth), 1.0 / math.s...  45.1 us
    unnamed x10, local copies, waits for them, and re-layouts  5.52 us

profile of v1, /device:TPU:0, one launch (start us, length us, event | category | flops | bytes accessed | tf_op | source)
XLA Modules:
  0.0 51.3 jit_solution(5683478723603385007)
XLA Ops:
  0.6 45.1 %block_step.1 = (f32[4,4,96,128]{3,2,1,0:T(8,128)}, f32[4,4,96,128]{3,2,1,0:T(8,128)}, f32[96,1296]{1,0:T(8,128)}, f32[96,1296]{1,0:T(8,128)}) custom-call(bf16[4,4,96,128]{3,2,1,0:T(8,128)(2,1)} %bitcast.14, bf16[4,4,96,128]{3,2,1,0:T(8,128)(2,1)} %bitcast.15, bf16[96,2592]{1,0:T(8,128)(2,1)} %bitcast.12, bf16[96,2592]{1,0:T(8,128)(2,1)} %bitcast.13), custom_call_target="tpu_custom_call" | custom-call | tf_op jit(solution)/shard_map/block_step/pallas_call | solution.py:512
  45.7 0.0 copy-start
  45.7 2.1 %copy.12 = f32[1,4,4,96,128]{4,3,2,1,0:T(8,128)} copy(f32[1,4,4,96,128]{4,3,2,1,0:T(8,128)} %bitcast.9) | data formatting | bytes 1572864
  47.9 0.0 copy-done
  47.9 0.0 copy-start.2
  47.9 0.9 %copy.13 = f32[1,4,4,96,128]{4,3,2,1,0:T(8,128)} copy(f32[1,4,4,96,128]{4,3,2,1,0:T(8,128)S(1)} %bitcast.8) | data formatting | bytes 1572864
  48.8 0.4 copy-done.2
  49.2 0.0 copy-start.1
  49.2 0.8 %copy.14 = f32[1296,96]{0,1:T(8,128)} copy(f32[1296,96]{0,1:T(8,128)S(1)} %bitcast.11) | data formatting | bytes 995328
  50.0 0.4 copy-done.1
  50.5 0.8 %copy.15 = f32[1296,96]{0,1:T(8,128)} copy(f32[1296,96]{0,1:T(8,128)S(1)} %bitcast.10) | data formatting | bytes 995328
Async XLA Ops:
  45.7 2.2 %copy-start = (f32[4,4,96,128]{3,2,1,0:T(8,128)S(1)}, f32[4,4,96,128]{3,2,1,0:T(8,128)}, u32[]{:S(2)}) copy-start(f32[4,4,96,128]{3,2,1,0:T(8,128)} %get-tuple-element.9) | copy-start | bytes 2359300
  47.9 1.3 %copy-start.2 = (f32[96,1296]{1,0:T(8,128)S(1)}, f32[96,1296]{1,0:T(8,128)}, u32[]{:S(2)}) copy-start(f32[96,1296]{1,0:T(8,128)} %get-tuple-element.10) | copy-start | bytes 1492996
  49.2 1.2 %copy-start.1 = (f32[96,1296]{1,0:T(8,128)S(1)}, f32[96,1296]{1,0:T(8,128)}, u32[]{:S(2)}) copy-start(f32[96,1296]{1,0:T(8,128)} %get-tuple-element.11) | copy-start | bytes 1492996

commit v2 on v1

--- a/solution.py
+++ b/solution.py
@@ -10,6 +10,7 @@
 
 EPSILON = 1e-06
 MESH_IDS = pl.DeviceIdType.MESH
+VMEM_BYTES = 40 << 20
 
 
 def factor_of(value):
@@ -65,9 +66,6 @@
     wide,
     narrow,
     plane_in,
-    wide_half,
-    narrow_half,
-    half_in,
     wide_z,
     narrow_z,
     got_z,
@@ -100,6 +98,9 @@
     places += [{"dp": peer} for peer in clip_peers]
     places += [{"tm": peer * 2 + core} for peer in level_peers]
 
+    plane_peers = [(peer, owner) for owner in (half, other) for peer in clip_peers] + [(clip, other)]
+    places += [{"dp": peer, "height": other} for peer in clip_peers]
+
     def greet(place):
         pl.semaphore_signal(barrier, inc=1, device_id=place, device_id_type=MESH_IDS)
 
@@ -353,65 +354,38 @@
         for copy in copies:
             copy.wait()
 
-    def reduce(index, plane_first):
+    def reduce(index):
         share = channels // 2
 
-        def piece_of(piece, line, owner):
-            lines = pl.ds(pl.multiple_of(owner * share + line * band, band), band)
-            return terms[index, piece, lines]
+        def lines_of(owner, line):
+            return pl.ds(pl.multiple_of(owner * share + line * band, band), band)
 
         for piece in range(dp):
             for line in range(2):
-                value = piece_of(piece, line, 1 - core).astype(jnp.bfloat16)
-                for block in range(depth):
-                    swap_out[index, piece, line, block] = value[:, block * width : (block + 1) * width]
+                swap_out[index, piece, line] = terms[index, piece, lines_of(1 - core, line)].astype(jnp.bfloat16)
         swap = send_to(swap_out.at[index], swap_in.at[index], partner)
         yield
         swap.wait()
         for piece in range(dp):
             for line in range(2):
-                value = piece_of(piece, line, core)
-                for block in range(depth):
-                    summed = value[:, block * width : (block + 1) * width]
-                    summed = summed + swap_in[index, piece, line, block].astype(jnp.float32)
-                    wide[index, piece, line, block] = summed
-                    narrow[index, piece, line, block] = summed.astype(jnp.bfloat16)
-        if plane_first:
-            copies = [
-                send_to(narrow.at[index, peer], plane_in.at[index, i], {"dp": peer}) for i, peer in enumerate(clip_peers)
-            ]
-            yield
-            wait_all(copies)
-            summed = wide[index, clip]
-            for i in range(dp - 1):
-                summed = summed + plane_in[index, i].astype(jnp.float32)
-            wide_half[index, 0:2] = summed
-            narrow_half[index, 0:2] = summed.astype(jnp.bfloat16)
-            copy = send_to(narrow_half.at[index, other], half_in.at[index, 0], {"height": other})
-            yield
-            copy.wait()
-            summed = wide_half[index, half] + half_in[index, 0].astype(jnp.float32)
-        else:
-            copies = [
-                send_to(narrow.at[index, piece, other], half_in.at[index, piece], {"height": other}) for piece in range(dp)
-            ]
-            yield
-            wait_all(copies)
-            for piece in range(dp):
-                summed = wide[index, piece, half] + half_in[index, piece].astype(jnp.float32)
-                wide_half[index, piece] = summed
-                narrow_half[index, piece] = summed.astype(jnp.bfloat16)
-            copies = [
-                send_to(narrow_half.at[index, peer], plane_in.at[index, i, 0], {"dp": peer})
-                for i, peer in enumerate(clip_peers)
-            ]
-            yield
-            wait_all(copies)
-            summed = wide_half[index, clip]
-            for i in range(dp - 1):
-                summed = summed + plane_in[index, i, 0].astype(jnp.float32)
-        wide_z[index] = summed
-        narrow_z[index] = summed.astype(jnp.bfloat16)
+                summed = terms[index, piece, lines_of(core, line)] + swap_in[index, piece, line].astype(jnp.float32)
+                wide[index, piece, line] = summed
+                narrow[index, piece, line] = summed.astype(jnp.bfloat16)
+        copies = [
+            send_to(narrow.at[index, places[0], places[1]], plane_in.at[index, i], {"dp": places[0], "height": places[1]})
+            for i, places in enumerate(plane_peers)
+        ]
+        yield
+        wait_all(copies)
+        summed = wide[index, clip, half]
+        for i in range(len(plane_peers)):
+            summed = summed + plane_in[index, i].astype(jnp.float32)
+        for block in range(depth):
+            start, stop = block * width, min((block + 1) * width, summed.shape[1])
+            if start < stop:
+                value = summed[:, start:stop]
+                wide_z[index, block, :, : stop - start] = value
+                narrow_z[index, block, :, : stop - start] = value.astype(jnp.bfloat16)
         copies = [
             send_to(narrow_z.at[index, peer], got_z.at[index, i], {"tm": peer * 2 + core})
             for i, peer in enumerate(level_peers)
@@ -423,17 +397,26 @@
             summed = summed + got_z[index, i].astype(jnp.float32)
         mine[index, core, half, level] = summed.astype(jnp.bfloat16)
         own = mine.at[index, core, half, level]
-        copies = [send_to(own, own, {"tm": peer * 2 + core}) for peer in level_peers]
+        along = [send_to(own, own, {"tm": peer * 2 + core}) for peer in level_peers]
+        across, inside = [], []
+
+        def pass_on(owner, step, targets):
+            block = mine.at[index, core, owner, (level + depth - step) % depth]
+            for copies, place in targets:
+                copies.append(send_to(block, block, place))
+
+        both = ((across, {"height": other}), (inside, partner))
+        pass_on(half, 0, both)
         yield
-        wait_all(copies)
-        own = mine.at[index, core, half]
-        copy = send_to(own, own, {"height": other})
+        for step in range(1, depth):
+            along[step - 1].wait()
+            pass_on(half, step, both)
         yield
-        copy.wait()
-        own = mine.at[index, core]
-        copy = send_to(own, own, partner)
+        for step in range(depth):
+            across[step].wait()
+            pass_on(other, step, both[1:])
         yield
-        copy.wait()
+        wait_all(inside)
         for place in range(2):
             for line in range(2):
                 top = place * share + line * band
@@ -458,7 +441,7 @@
             copies_out.append(bring(input_own.at[frame], input_out.at[frame]))
 
     kernel_grad(0, acts_one, middle_grad)
-    first = reduce(0, True)
+    first = reduce(0)
     next(first)
     act_rows()
     fill_rows(acts_two, 2, False, same)
@@ -466,30 +449,36 @@
     fill_time(acts_two, 2, False, same)
     kernel_grad(1, acts_two, cot_own)
     next(first)
-    second = reduce(1, False)
+    second = reduce(1)
     next(second)
     steps = conv(acts_two, ahead_weights[1], range(frames + 2), finish_branch)
     run(steps[:3])
     next(second)
     run(steps[3:])
-    next(first)
     grad_rows()
     fill_rows(grads_one, 3, True, same)
     grad_time()
     fill_time(grads_one, 3, True, same)
+    next(first)
     steps = conv(grads_one, back_weights[0], range(frames + 2), finish_input)
-    run(steps[:2])
+    run(steps[:3])
     next(second)
-    run(steps[2:4])
-    next(first)
-    run(steps[4:])
-    next(second)
+    run(steps[3:])
     going = [first, second]
     while going:
         for task in list(going):
             if next(task, 0) == 0:
                 going.remove(task)
     wait_all(copies_out)
+
+
+def deliver(*refs):
+    count = len(refs) // 2
+    copies = [pltpu.make_async_copy(refs[i], refs[count + i], refs[-1].at[i]) for i in range(count)]
+    for copy in copies:
+        copy.start()
+    for copy in copies:
+        copy.wait()
 
 
 def local(clip_input, cotangent, first_kernel, second_kernel):
@@ -500,7 +489,8 @@
     chunk = taps // dp
     band = channels // 4
     width = -(-chunk // (cols * depth)) * cols
-    sends = 2 * (1 + (dp - 1) + max(1, dp) + 2 * (depth - 1) + 2)
+    lanes = -(-chunk // cols) * cols
+    sends = 2 * (1 + (2 * dp - 1) + 2 * (depth - 1) + 3 * depth)
     tile = (channels, cols)
     own = (frames, rows) + tile
     block = (depth, band, width)
@@ -509,7 +499,7 @@
     padded = pltpu.VMEM((frames + 4, rows) + tile, jnp.bfloat16)
     weights = pltpu.VMEM((2, 3 * channels, 9 * channels), jnp.bfloat16)
     positions = frames * rows * cols * dp * heights * lax.axis_size("tm")
-    block_output, input_grad, grad_one, grad_two = pl.pallas_call(
+    found = pl.pallas_call(
         functools.partial(body, (dp, heights, depth), 1.0 / math.sqrt(positions)),
         out_shape=(
             jax.ShapeDtypeStruct(own, jnp.float32),
@@ -517,7 +507,7 @@
             jax.ShapeDtypeStruct((channels, chunk), jnp.float32),
             jax.ShapeDtypeStruct((channels, chunk), jnp.float32),
         ),
-        in_specs=[anywhere] * 4,
+        in_specs=[pl.BlockSpec(memory_space=pltpu.HBM)] * 4,
         out_specs=(anywhere,) * 4,
         scratch_shapes=[
             pltpu.VMEM(own, jnp.bfloat16),
@@ -539,15 +529,12 @@
             pltpu.VMEM((4, 2, rows) + tile, jnp.bfloat16),
             pltpu.VMEM((4, frames) + tile, jnp.bfloat16),
             pltpu.VMEM((4, 2) + tile, jnp.bfloat16),
-            pltpu.VMEM((2, dp, channels, depth * width), jnp.float32),
-            pltpu.VMEM((2, dp, 2) + block, jnp.bfloat16),
-            pltpu.VMEM((2, dp, 2) + block, jnp.bfloat16),
-            pltpu.VMEM((2, dp, 2) + block, jnp.float32),
-            pltpu.VMEM((2, dp, 2) + block, jnp.bfloat16),
-            pltpu.VMEM((2, dp - 1, 2) + block, jnp.bfloat16),
-            pltpu.VMEM((2, max(2, dp)) + block, jnp.float32),
-            pltpu.VMEM((2, max(2, dp)) + block, jnp.bfloat16),
-            pltpu.VMEM((2, dp) + block, jnp.bfloat16),
+            pltpu.VMEM((2, dp, channels, lanes), jnp.float32),
+            pltpu.VMEM((2, dp, 2, band, lanes), jnp.bfloat16),
+            pltpu.VMEM((2, dp, 2, band, lanes), jnp.bfloat16),
+            pltpu.VMEM((2, dp, 2, band, lanes), jnp.float32),
+            pltpu.VMEM((2, dp, 2, band, lanes), jnp.bfloat16),
+            pltpu.VMEM((2, 2 * dp - 1, band, lanes), jnp.bfloat16),
             pltpu.VMEM((2,) + block, jnp.float32),
             pltpu.VMEM((2,) + block, jnp.bfloat16),
             pltpu.VMEM((2, depth - 1, band, width), jnp.bfloat16),
@@ -558,9 +545,20 @@
             pltpu.SemaphoreType.DMA((sends,)),
             pltpu.SemaphoreType.DMA((6 + 2 * frames,)),
         ],
-        compiler_params=pltpu.CompilerParams(collective_id=0, has_side_effects=True),
+        compiler_params=pltpu.CompilerParams(
+            collective_id=0, has_side_effects=True, vmem_limit_bytes=VMEM_BYTES
+        ),
         name="block_step",
-    )(clip_input[0], cotangent[0], first_kernel.T, second_kernel.T)
+    )(*[pltpu.with_memory_space_constraint(value, pltpu.HBM) for value in (clip_input[0], cotangent[0], first_kernel.T, second_kernel.T)])
+    block_output, input_grad, grad_one, grad_two = pl.pallas_call(
+        deliver,
+        out_shape=[jax.ShapeDtypeStruct(value.shape, value.dtype) for value in found],
+        in_specs=[anywhere] * len(found),
+        out_specs=[anywhere] * len(found),
+        scratch_shapes=[pltpu.SemaphoreType.DMA((len(found),))],
+        compiler_params=pltpu.CompilerParams(vmem_limit_bytes=1 << 20),
+        name="deliver",
+    )(*found)
     return (block_output[None], input_grad[None], grad_one.T, grad_two.T)
 
 

time: 51.5 us -> 43.3 us (0.84)
  local copies, waits for them, and re-layouts: 5.52 us -> 0 us
  Pallas kernels: 45.1 us -> 42.6 us
    unnamed x10 -> x0, local copies, waits for them, and re-layouts: 5.52 us -> none
    pallas_call x1, Pallas kernels: 45.1 us -> 41 us  [local(): pl.pallas_call(functools.partial(body, (dp, heights, depth), 1.0 / math.s...]
    pallas_call x0 -> x1, Pallas kernels: none -> 1.53 us  [local(): pl.pallas_call(deliver, out_shape=[jax.ShapeDtypeStruct(value.shape, valu...]
where the time goes in v2:
time: 43.3 us; the launch traced here: 43.2 us
  Pallas kernels  42.6 us (98%)
  between operations  0.64 us (1%)
    pallas_call x1, Pallas kernels, local(): pl.pallas_call(functools.partial(body, (dp, heights, depth), 1.0 / math.s...  41 us
    pallas_call x1, Pallas kernels, local(): pl.pallas_call(deliver, out_shape=[jax.ShapeDtypeStruct(value.shape, valu...  1.53 us

profile of v2, /device:TPU:0, one launch (start us, length us, event | category | flops | bytes accessed | tf_op | source)
XLA Modules:
  0.0 43.2 jit_solution(13321438571578952947)
XLA Ops:
  0.6 41.0 %block_step.1 = (f32[4,4,96,128]{3,2,1,0:T(8,128)S(1)}, f32[4,4,96,128]{3,2,1,0:T(8,128)S(1)}, f32[96,1296]{1,0:T(8,128)S(1)}, f32[96,1296]{1,0:T(8,128)S(1)}) custom-call(bf16[4,4,96,128]{3,2,1,0:T(8,128)(2,1)} %bitcast.10, bf16[4,4,96,128]{3,2,1,0:T(8,128)(2,1)} %bitcast.11, bf16[96,2592]{1,0:T(8,128)(2,1)} %bitcast.8, bf16[96,2592]{1,0:T(8,128)(2,1)} %bitcast.9), custom_call_target="tpu_custom_call" | custom-call | tf_op jit(solution)/shard_map/block_step/pallas_call | solution.py:502
  41.7 1.5 %deliver.1 = (f32[4,4,96,128]{3,2,1,0:T(8,128)}, f32[4,4,96,128]{3,2,1,0:T(8,128)}, f32[96,1296]{1,0:T(8,128)}, f32[96,1296]{1,0:T(8,128)}) custom-call(f32[4,4,96,128]{3,2,1,0:T(8,128)S(1)} %get-tuple-element.12.refs_0_, f32[4,4,96,128]{3,2,1,0:T(8,128)S(1)} %get-tuple-element.13.refs_1_, f32[96,1296]{1,0:T(8,128)S(1)} %get-tuple-element.14.refs_2_, ...), custom_call_target="tpu_custom_call" | custom-call | tf_op jit(solution)/shard_map/deliver/pallas_call | solution.py:553

commit v3 on v2

--- a/solution.py
+++ b/solution.py
@@ -186,8 +186,6 @@
     cot_rows_go, cot_time_goes, cot_rows, cot_time = exchange(cot, 1, True)
     x_rows_go()
     x_time_goes()
-    cot_rows_go()
-    cot_time_goes()
 
     lane = lax.broadcasted_iota(jnp.int32, (channels, cols), 1)
 
@@ -315,6 +313,8 @@
         place_tile(acts_two, frame + 2, row + 1, rounded)
 
     act_rows_go, act_time_goes, act_rows, act_time = exchange(second_act, 2, False)
+    cot_rows_go()
+    cot_time_goes()
     x_rows()
     fill_rows(acts_one, 0, False, as_act)
     steps = conv(acts_one, ahead_weights[0], range(frames + 1, -1, -1), finish_middle)

time: 43.3 us -> 43.1 us (level)
  no operation moved by 1% of the time
where the time goes in v3:
time: 43.1 us; the launch traced here: 43 us
  Pallas kernels  42.3 us (98%)
  between operations  0.64 us (1%)
    pallas_call x1, Pallas kernels, local(): pl.pallas_call(functools.partial(body, (dp, heights, depth), 1.0 / math.s...  40.8 us
    pallas_call x1, Pallas kernels, local(): pl.pallas_call(deliver, out_shape=[jax.ShapeDtypeStruct(value.shape, valu...  1.53 us

profile of v3, /device:TPU:0, one launch (start us, length us, event | category | flops | bytes accessed | tf_op | source)
XLA Modules:
  0.0 43.0 jit_solution(9292909707699723051)
XLA Ops:
  0.6 40.8 %block_step.1 = (f32[4,4,96,128]{3,2,1,0:T(8,128)S(1)}, f32[4,4,96,128]{3,2,1,0:T(8,128)S(1)}, f32[96,1296]{1,0:T(8,128)S(1)}, f32[96,1296]{1,0:T(8,128)S(1)}) custom-call(bf16[4,4,96,128]{3,2,1,0:T(8,128)(2,1)} %bitcast.10, bf16[4,4,96,128]{3,2,1,0:T(8,128)(2,1)} %bitcast.11, bf16[96,2592]{1,0:T(8,128)(2,1)} %bitcast.8, bf16[96,2592]{1,0:T(8,128)(2,1)} %bitcast.9), custom_call_target="tpu_custom_call" | custom-call | tf_op jit(solution)/shard_map/block_step/pallas_call | solution.py:502
  41.4 1.5 %deliver.1 = (f32[4,4,96,128]{3,2,1,0:T(8,128)}, f32[4,4,96,128]{3,2,1,0:T(8,128)}, f32[96,1296]{1,0:T(8,128)}, f32[96,1296]{1,0:T(8,128)}) custom-call(f32[4,4,96,128]{3,2,1,0:T(8,128)S(1)} %get-tuple-element.12.refs_0_, f32[4,4,96,128]{3,2,1,0:T(8,128)S(1)} %get-tuple-element.13.refs_1_, f32[96,1296]{1,0:T(8,128)S(1)} %get-tuple-element.14.refs_2_, ...), custom_call_target="tpu_custom_call" | custom-call | tf_op jit(solution)/shard_map/deliver/pallas_call | solution.py:553

commit v4 on v3

--- a/solution.py
+++ b/solution.py
@@ -405,16 +405,20 @@
             for copies, place in targets:
                 copies.append(send_to(block, block, place))
 
-        both = ((across, {"height": other}), (inside, partner))
+        def pass_inside(owner):
+            region = mine.at[index, core, owner]
+            inside.append(send_to(region, region, partner))
+
+        both = ((across, {"height": other}),)
         pass_on(half, 0, both)
         yield
         for step in range(1, depth):
             along[step - 1].wait()
             pass_on(half, step, both)
+        pass_inside(half)
         yield
-        for step in range(depth):
-            across[step].wait()
-            pass_on(other, step, both[1:])
+        wait_all(across)
+        pass_inside(other)
         yield
         wait_all(inside)
         for place in range(2):

time: 43.1 us -> 43.2 us (level)
  no operation moved by 1% of the time
where the time goes in v4:
time: 43.2 us; the launch traced here: 43.1 us
  Pallas kernels  42.4 us (98%)
  between operations  0.64 us (1%)
    pallas_call x1, Pallas kernels, local(): pl.pallas_call(functools.partial(body, (dp, heights, depth), 1.0 / math.s...  40.9 us
    pallas_call x1, Pallas kernels, local(): pl.pallas_call(deliver, out_shape=[jax.ShapeDtypeStruct(value.shape, valu...  1.53 us

profile of v4, /device:TPU:0, one launch (start us, length us, event | category | flops | bytes accessed | tf_op | source)
XLA Modules:
  0.0 43.1 jit_solution(3654109920232672440)
XLA Ops:
  0.6 40.9 %block_step.1 = (f32[4,4,96,128]{3,2,1,0:T(8,128)S(1)}, f32[4,4,96,128]{3,2,1,0:T(8,128)S(1)}, f32[96,1296]{1,0:T(8,128)S(1)}, f32[96,1296]{1,0:T(8,128)S(1)}) custom-call(bf16[4,4,96,128]{3,2,1,0:T(8,128)(2,1)} %bitcast.10, bf16[4,4,96,128]{3,2,1,0:T(8,128)(2,1)} %bitcast.11, bf16[96,2592]{1,0:T(8,128)(2,1)} %bitcast.8, bf16[96,2592]{1,0:T(8,128)(2,1)} %bitcast.9), custom_call_target="tpu_custom_call" | custom-call | tf_op jit(solution)/shard_map/block_step/pallas_call | solution.py:506
  41.5 1.5 %deliver.1 = (f32[4,4,96,128]{3,2,1,0:T(8,128)}, f32[4,4,96,128]{3,2,1,0:T(8,128)}, f32[96,1296]{1,0:T(8,128)}, f32[96,1296]{1,0:T(8,128)}) custom-call(f32[4,4,96,128]{3,2,1,0:T(8,128)S(1)} %get-tuple-element.12.refs_0_, f32[4,4,96,128]{3,2,1,0:T(8,128)S(1)} %get-tuple-element.13.refs_1_, f32[96,1296]{1,0:T(8,128)S(1)} %get-tuple-element.14.refs_2_, ...), custom_call_target="tpu_custom_call" | custom-call | tf_op jit(solution)/shard_map/deliver/pallas_call | solution.py:557
